TPU v7x, 32 devices: a whole 2x2x4 slice. The times are simulated.
32 devices in a mesh: fsdp: 4 (over y, x), ctx: 8 (over z, core).
Axes of the slice: x: 2, y: 2, z: 4, core: 2. Of those that a mesh axis runs over, the one named last changes fastest.
Arguments:
- tokens: bfloat16 [4, 1024, 5376], P('fsdp', 'ctx'), may hold values from -6 to 6
- pre_gain: float32 [5376], replicated, may hold values from 0.1 to 1.9
- w_query: bfloat16 [5376, 3072], P(None, 'fsdp'), may hold values from -0.078125 to 0.078125
- key_weight: bfloat16 [5376, 1536], P(None, 'fsdp'), may hold values from -0.078125 to 0.078125
- value_weight: bfloat16 [5376, 1536], P(None, 'fsdp'), may hold values from -0.078125 to 0.078125
- query_norm_gain: float32 [128], replicated, may hold values from 0.1 to 1.9
- key_gain: float32 [128], replicated, may hold values from 0.1 to 1.9
- w_out: bfloat16 [3072, 5376], P('fsdp'), may hold values from -0.109375 to 0.109375
- post_gain: float32 [5376], replicated, may hold values from 0.1 to 1.9
Outputs:
- layer_out: bfloat16 [4, 1024, 5376], P('fsdp', 'ctx')
All inputs are finite; a program needn't handle non-finite values.
Results may differ from a plain program's by a relative error of at most 0.012.
Values may be sent and summed in bfloat16 or wider, within the bound.
A program may use at most 128 MiB of HBM per device.

v0:
```python
import functools
import math

import jax
import jax.numpy as jnp
from jax import lax
from jax.experimental import pallas as pl
from jax.experimental.pallas import tpu as pltpu
from jax.sharding import PartitionSpec as P

epsilon = 1e-06
score_scale = 168.0 ** (-0.5)
window = 1024
vmem_limit = 58_000_000
MESH = pl.DeviceIdType.MESH
halves_of = ((0, 0), (1, 2), (2, 1), (3, 3))


def column_step(total, limit):
    step = 128
    for count in range(1, limit // 128 + 1):
        if total % (count * 128) == 0:
            step = count * 128
    return step


def layer_kernel(
    n_ctx, reach, q_heads, kv_heads, head,
    tok_hbm, wq_hbm, wk_hbm, wv_hbm, wo_hbm, pre_ref, post_ref, qg_ref, kg_ref, cos_ref, sin_ref,
    out_ref,
    tok, w, wo, nb, raw, q, kv, att, pb, rx, ry, dg, pre, post, accs, sums,
    load_sem, ag_s, ag_r, rs_s, rs_r, z_s, z_r, b_s, b_r,
):
    f = lax.axis_index("fsdp")
    c = lax.axis_index("ctx")
    rows, features = tok.shape
    half = rows // 2
    z = c // 2
    p = c % 2
    nz = n_ctx // 2
    x_to = {"fsdp": f + 1 - 2 * (f % 2)}
    y_to = {"fsdp": (f + 2) % 4}
    sib = {"ctx": c + 1 - 2 * p}

    def ahead(step):
        return {"ctx": lax.rem(c + 2 * step, n_ctx)}, z + step < nz

    def behind(step):
        return {"ctx": lax.rem(c + n_ctx - 2 * step, n_ctx)}, z >= step

    direct = [step for step in (1, 3) if step <= reach]
    qw, kw = q_heads * head, kv_heads * head
    group = q_heads // kv_heads

    def load(i, src, dst):
        return pltpu.make_async_copy(src, dst, load_sem.at[i])

    tok_loads = [load(i, tok_hbm.at[pl.ds(i * half, half)], tok.at[pl.ds(i * half, half)]) for i in range(2)]
    for d in tok_loads:
        d.start()
    loads = []
    cut = features // 2
    for j, (src, lo, wide) in enumerate(((wk_hbm, qw, kw), (wv_hbm, qw + kw, kw), (wq_hbm, 0, qw))):
        for part in range(2):
            rs = pl.ds(part * cut, cut)
            loads.append(load(2 + 2 * j + part, src.at[rs], w.at[rs, pl.ds(lo, wide)]))
    wo_load = load(8, wo_hbm, wo)

    barrier = pltpu.get_barrier_semaphore()
    for to in (x_to, y_to, sib):
        pl.semaphore_signal(barrier, inc=1, device_id=to, device_id_type=MESH)

    peers = 3
    for step in direct:
        for to, there in (ahead(step), behind(step)):
            pl.when(there)(functools.partial(
                pl.semaphore_signal, barrier, inc=1, device_id=to, device_id_type=MESH
            ))
        peers = peers + jnp.clip(z - step + 1, 0, 1) + jnp.clip(nz - z - step, 0, 1)

    for wide, gain in ((pre, pre_ref), (post, post_ref)):
        wide[...] = jnp.concatenate([gain[k : k + 1, :] for k in range(gain.shape[0])], axis=1)
    tok_loads[0].wait()

    def norm_rows(i, carry):
        at = pl.ds(pl.multiple_of(i * 16, 16), 16)
        v = tok[at, :].astype(jnp.float32)
        mean_sq = jnp.mean(v * v, axis=-1, keepdims=True)
        nb[0, at, :] = (v * lax.rsqrt(mean_sq + epsilon) * pre[...]).astype(jnp.bfloat16)
        return carry

    lax.fori_loop(0, half // 16, norm_rows, 0)
    tok_loads[1].wait()
    for d in loads:
        d.start()
    wo_load.start()
    pl.semaphore_wait(barrier, peers)

    A, B = pl.ds(0, half), pl.ds(half, half)

    def remote(src, dst, s, r, to):
        return pltpu.make_async_remote_copy(
            src_ref=src, dst_ref=dst, send_sem=s, recv_sem=r, device_id=to, device_id_type=MESH
        )

    def ag(i):
        src, dst, to = (
            (nb.at[0, A], nb.at[1, A], x_to),
            (nb.at[0, B], nb.at[2, B], x_to),
            (nb.at[0, B], nb.at[1, B], y_to),
            (nb.at[0, A], nb.at[2, A], y_to),
            (nb.at[1, A], nb.at[3, A], y_to),
            (nb.at[1, B], nb.at[3, B], x_to),
        )[i]
        return remote(src, dst, ag_s.at[i], ag_r.at[i], to)

    ag(0).start()
    lax.fori_loop(half // 16, rows // 16, norm_rows, 0)
    for i in (2, 1, 3):
        ag(i).start()

    def z_copy(u, dz, step):
        return remote(
            kv.at[u, dz, p], kv.at[u, dz + step, p], z_s.at[u, dz + step], z_r.at[u, dz + step], ahead(step)[0]
        )

    def b_copy(u, dz):
        return remote(kv.at[u, dz, p], kv.at[u, dz, p], b_s.at[u, dz], b_r.at[u, dz], sib)

    def kv_arrived(u, dz):
        return remote(kv.at[u, dz, p], kv.at[u, dz, p], z_s.at[u, dz], z_r.at[u, dz], behind(1)[0])

    def kv_paired(u, dz):
        return remote(kv.at[u, dz, 1 - p], kv.at[u, dz, 1 - p], b_s.at[u, dz], b_r.at[u, dz], sib)

    def own_copies(u, act):
        for step in direct:
            @pl.when(ahead(step)[1])
            def _():
                act(z_copy(u, 0, step))

        @pl.when(p == 0)
        def _():
            act(b_copy(u, 0))

    def send_own(u):
        own_copies(u, lambda d: d.start())

    def passed_copies(u, dz, act):
        if dz in direct and dz + 1 <= reach:
            @pl.when(ahead(1)[1])
            def _():
                act(z_copy(u, dz, 1))

        act(b_copy(u, dz))

    def relay(u, dz):
        if dz > reach:
            return

        @pl.when(z >= dz)
        def _():
            kv_arrived(u, dz).wait_recv()
            passed_copies(u, dz, lambda d: d.start())

    def wait_pairs(u):
        @pl.when(p == 1)
        def _():
            kv_paired(u, 0).wait_recv()

        for dz in range(1, reach + 1):
            @pl.when(z >= dz)
            def _():
                kv_paired(u, dz).wait_recv()

    k_step = column_step(2 * kw, 256)
    q_step = column_step(qw, 256)

    def columns_of(u, first, count, step):
        def columns(j, carry):
            at = pl.ds(pl.multiple_of(first + j * step, 128), step)
            raw[:, at] = jnp.dot(nb[u], w[:, at], preferred_element_type=jnp.float32)
            return carry

        lax.fori_loop(0, count // step, columns, 0)

    def rotated(col, gain):
        v = raw[:, col : col + head]
        mean_sq = jnp.mean(v * v, axis=-1, keepdims=True)
        v = v * lax.rsqrt(mean_sq + epsilon) * gain[...]
        return (v * cos_ref[...] + pltpu.roll(v, head // 2, 1) * sin_ref[...]).astype(jnp.bfloat16)

    def project_keys(u):
        columns_of(u, qw, 2 * kw, k_step)
        for h in range(kv_heads):
            kv[u, 0, p, :, h * head : (h + 1) * head] = rotated(qw + h * head, kg_ref)
        kv[u, 0, p, :, kw:] = raw[:, qw + kw :].astype(jnp.bfloat16)

    def project_queries(u):
        columns_of(u, 0, qw, q_step)
        for h in range(q_heads):
            q[u, :, h * head : (h + 1) * head] = rotated(h * head, qg_ref)

    def merged(parts):
        return jnp.concatenate(parts, axis=0)

    def attend(u):
        own, other = halves_of[u], halves_of[(0, 2, 1, 3)[u]]
        spans = [(0, rows, own)] if own == other else [(0, half, own), (half, half, other)]
        streams = [
            (i * kv_heads + g, g, lo, size, units)
            for i, (lo, size, units) in enumerate(spans) for g in range(kv_heads)
        ]

        def places(lo, size):
            qi = lax.broadcasted_iota(jnp.int32, (group, size, rows), 1).reshape(group * size, rows) + lo
            return qi, lax.broadcasted_iota(jnp.int32, (group * size, rows), 1)

        def block(units, dz, par, cols):
            ua, ub = units
            if ua == ub:
                return kv[ua, dz, par, :, cols]
            return merged([kv[ua, dz, par, :half, cols], kv[ub, dz, par, half:, cols]])

        def step(dz, pars, mask, first=False):
            for n, g, lo, size, units in streams:
                kc = slice(g * head, (g + 1) * head)
                vc = slice(kw + g * head, kw + (g + 1) * head)
                at = slice(0, group * size)
                queries = merged([
                    q[u, lo : lo + size, h * head : (h + 1) * head] for h in range(g * group, (g + 1) * group)
                ])
                keys = merged([block(units, dz, par, kc) for par in pars])
                values = merged([block(units, dz, par, vc) for par in pars])
                s = lax.dot_general(queries, keys, (((1,), (1,)), ((), ())), preferred_element_type=jnp.float32)
                e = jnp.exp(s * score_scale)
                if mask is not None:
                    e = jnp.where(mask(lo, size), e, 0.0)
                total = sum(e[:, i * rows : (i + 1) * rows] for i in range(len(pars)))
                acc = jnp.dot(e.astype(jnp.bfloat16), values, preferred_element_type=jnp.float32)
                if first:
                    sums[n, at], accs[n, at] = total, acc
                else:
                    sums[n, at] += total
                    accs[n, at] += acc

        def causal(lo, size):
            qi, kj = places(lo, size)
            return kj <= qi

        step(0, [p], causal, True)

        def beside(_, carry):
            step(0, [0], None)
            return carry

        def earlier(dz, carry):
            def near(lo, size):
                qi, kj = places(lo, size)
                apart = (p + 2 * dz) * rows + qi - kj
                return jnp.concatenate([apart, apart - rows], axis=1) < window

            step(dz, [0, 1], near if n_ctx * rows > window else None)
            return carry

        lax.fori_loop(0, p, beside, 0)
        lax.fori_loop(1, jnp.minimum(z, reach) + 1, earlier, 0)
        for n, g, lo, size, _ in streams:
            at = slice(0, group * size)
            o = (accs[n, at] / jnp.sum(sums[n, at], axis=-1, keepdims=True)).astype(jnp.bfloat16)
            for i in range(group):
                h = g * group + i
                att[u, lo : lo + size, h * head : (h + 1) * head] = o[i * size : (i + 1) * size]

    o_step = column_step(features, 768)

    def output(u):
        def columns(j, carry):
            at = pl.ds(pl.multiple_of(j * o_step, o_step), o_step)
            pb[u, :, at] = jnp.dot(att[u], wo[:, at], preferred_element_type=jnp.float32).astype(jnp.bfloat16)
            return carry

        lax.fori_loop(0, features // o_step, columns, 0)

    quarter = half // 2
    A0, A1 = pl.ds(0, quarter), pl.ds(quarter, quarter)
    B0, B1 = pl.ds(half, quarter), pl.ds(half + quarter, quarter)

    def rs(i):
        src, dst, to = (
            (pb.at[1, A], rx.at[A], x_to),
            (pb.at[1, B], ry.at[B], y_to),
            (pb.at[3, A0], dg.at[A0], x_to),
            (pb.at[3, B0], dg.at[B0], y_to),
            (pb.at[3, A1], dg.at[A1], x_to),
            (pb.at[3, B1], dg.at[B1], y_to),
            (pb.at[2, A0], ry.at[A0], y_to),
            (pb.at[2, B0], rx.at[B0], x_to),
            (pb.at[2, A1], ry.at[A1], y_to),
            (pb.at[2, B1], rx.at[B1], x_to),
        )[i]
        return remote(src, dst, rs_s.at[i], rs_r.at[i], to)

    for d in loads:
        d.wait()
    project_keys(0)
    ag(0).wait_recv()
    ag(4).start()
    ag(2).wait_recv()
    ag(5).start()
    project_keys(1)
    send_own(1)
    project_queries(1)
    relay(1, 1)
    project_queries(0)
    ag(1).wait_recv()
    ag(3).wait_recv()
    project_keys(2)
    send_own(2)
    for dz in range(2, reach + 1):
        relay(1, dz)
    project_queries(2)
    relay(2, 1)
    relay(2, 2)
    ag(4).wait_recv()
    ag(5).wait_recv()
    project_keys(3)
    send_own(3)
    for dz in range(3, reach + 1):
        relay(2, dz)
    wo_load.wait()
    wait_pairs(1)
    wait_pairs(2)
    attend(1)
    output(1)
    rs(0).start()
    rs(1).start()
    relay(3, 1)
    attend(2)
    project_queries(3)
    for dz in range(2, reach + 1):
        relay(3, dz)
    send_own(0)
    wait_pairs(3)
    attend(3)
    output(3)
    for i in (2, 3, 4, 5):
        rs(i).start()
    output(2)
    relay(0, 1)

    def add_rows(first, count):
        def body(i, carry):
            at = pl.ds(pl.multiple_of(first + i * 16, 16), 16)
            pb[2, at, :] = (pb[2, at, :].astype(jnp.float32) + dg[at, :].astype(jnp.float32)).astype(jnp.bfloat16)
            return carry

        lax.fori_loop(0, count // 16, body, 0)

    for i, first in ((2, 0), (3, half), (4, quarter), (5, half + quarter)):
        rs(i).wait_recv()
        add_rows(first, quarter)
        rs(i + 4).start()
    for dz in range(2, reach + 1):
        relay(0, dz)
    wait_pairs(0)
    attend(0)
    output(0)

    def finish(first, count):
        def body(i, carry):
            at = pl.ds(pl.multiple_of(first + i * 16, 16), 16)
            summed = pb[0, at, :].astype(jnp.float32) + rx[at, :].astype(jnp.float32) + ry[at, :].astype(jnp.float32)
            mean_sq = jnp.mean(summed * summed, axis=-1, keepdims=True)
            normed = summed * lax.rsqrt(mean_sq + epsilon) * post[...]
            out_ref[at, :] = (tok[at, :].astype(jnp.float32) + normed).astype(jnp.bfloat16)
            return carry

        lax.fori_loop(0, count // 16, body, 0)

    rs(0).wait_recv()
    rs(1).wait_recv()
    for i, first in ((6, 0), (7, half), (8, quarter), (9, half + quarter)):
        rs(i).wait_recv()
        finish(first, quarter)

    for i in range(6):
        ag(i).wait_send()
    for i in range(10):
        rs(i).wait_send()
    for u in range(4):
        own_copies(u, lambda d: d.wait_send())
        for dz in range(1, reach + 1):
            @pl.when(z >= dz)
            def _():
                passed_copies(u, dz, lambda d: d.wait_send())


def per_device(
    n_ctx, tokens, pre_gain, w_query, key_weight, value_weight, query_norm_gain, key_gain, w_out, post_gain
):
    _, rows, features = tokens.shape
    head = query_norm_gain.shape[0]
    qw, kw = w_query.shape[1], key_weight.shape[1]
    reach = min(n_ctx // 2 - 1, -(-window // (2 * rows)))
    half_dim = head // 2
    positions = lax.axis_index("ctx") * rows + jnp.arange(rows, dtype=jnp.int32)
    frequencies = 10000.0 ** (-jnp.arange(half_dim, dtype=jnp.float32) / half_dim)
    angles = positions.astype(jnp.float32)[:, None] * frequencies[None, :]
    cosine, sine = jnp.cos(angles), jnp.sin(angles)
    cos_all = jnp.concatenate([cosine, cosine], axis=1)
    sin_all = jnp.concatenate([-sine, sine], axis=1)
    any_spec = pl.BlockSpec(memory_space=pl.ANY)
    vmem_spec = pl.BlockSpec(memory_space=pltpu.VMEM)
    bf16 = jnp.bfloat16
    dma = pltpu.SemaphoreType.DMA
    out = pl.pallas_call(
        functools.partial(layer_kernel, n_ctx, reach, qw // head, kw // head, head),
        out_shape=jax.ShapeDtypeStruct((rows, features), bf16),
        in_specs=[any_spec] * 5 + [vmem_spec] * 6,
        out_specs=vmem_spec,
        scratch_shapes=[
            pltpu.VMEM((rows, features), bf16),
            pltpu.VMEM((features, qw + 2 * kw), bf16),
            pltpu.VMEM((qw, features), bf16),
            pltpu.VMEM((4, rows, features), bf16),
            pltpu.VMEM((rows, qw + 2 * kw), jnp.float32),
            pltpu.VMEM((4, rows, qw), bf16),
            pltpu.VMEM((4, reach + 1, 2, rows, 2 * kw), bf16),
            pltpu.VMEM((4, rows, qw), bf16),
            pltpu.VMEM((4, rows, features), bf16),
            pltpu.VMEM((rows, features), bf16),
            pltpu.VMEM((rows, features), bf16),
            pltpu.VMEM((rows, features), bf16),
            pltpu.VMEM((1, features), jnp.float32),
            pltpu.VMEM((1, features), jnp.float32),
            pltpu.VMEM((2 * kw // head, qw // kw * rows, head), jnp.float32),
            pltpu.VMEM((2 * kw // head, qw // kw * rows, rows), jnp.float32),
            dma((9,)), dma((6,)), dma((6,)), dma((10,)), dma((10,)),
            dma((4, reach + 1)), dma((4, reach + 1)), dma((4, reach + 1)), dma((4, reach + 1)),
        ],
        compiler_params=pltpu.CompilerParams(
            collective_id=0, has_side_effects=True, vmem_limit_bytes=vmem_limit
        ),
    )(
        tokens[0], w_query, key_weight, value_weight, w_out,
        pre_gain.reshape(-1, 128), post_gain.reshape(-1, 128), query_norm_gain[None], key_gain[None], cos_all, sin_all,
    )
    return out[None]


def solution(mesh):
    return jax.shard_map(
        functools.partial(per_device, mesh.shape["ctx"]),
        mesh=mesh,
        in_specs=(
            P("fsdp", "ctx", None),
            P(),
            P(None, "fsdp"),
            P(None, "fsdp"),
            P(None, "fsdp"),
            P(),
            P(),
            P("fsdp", None),
            P(),
        ),
        out_specs=P("fsdp", "ctx", None),
        check_vma=False,
    )
```

profile of v0, /device:TPU:24, one launch (start us, length us, event | category | flops | bytes accessed | tf_op | source)
XLA Modules:
  0.0 110.9 jit_solution(84699237063086243)
XLA Ops:
  0.0 0.3 fusion
  0.3 0.7 pad_maximum_fusion
  1.1 107.3 %shard_map.91 = bf16[128,5376]{1,0:T(8,128)(2,1)} custom-call(bf16[128,5376]{1,0:T(8,128)(2,1)} %bitcast.7, bf16[5376,768]{1,0:T(8,128)(2,1)} %wq_hbm.1, bf16[5376,384]{1,0:T(8,128)(2,1)} %wk_hbm.1, bf16[5376,384]{1,0:T(8,128)(2,1)} %wv_hbm.1, bf16[768,5376]{1,0:T(8,128)(2,1)} %wo_hbm.1, f32[42,128]{1,0:T(8,128)} %bitcast.8, f32[42,128]{1,0:T(8,128)} %bitcast.9, ...), custom_call_target="tpu_custom_call" | custom-call | tf_op jit(solution)/shard_map/pallas_call | solution.py:417
  108.4 2.5 %copy.11 = bf16[1,128,5376]{2,1,0:T(8,128)(2,1)} copy(bf16[1,128,5376]{2,1,0:T(8,128)(2,1)} %bitcast.6) | data formatting | bytes 2752512
  (2 shorter events, 0.0 us)
where the time goes:
time: 111 us
  Pallas kernels  107 us (96%)
  local copies, waits for them, and re-layouts  2.51 us (2%)
    pallas_call x1, Pallas kernels, per_device(): pl.pallas_call(functools.partial(layer_kernel, n_ctx, reach, qw // head,...  107 us
    unnamed x1, local copies, waits for them, and re-layouts  2.51 us

commit v1 on v0

v1 whole, which is shorter than its diff:
```python
import functools
import math

import jax
import jax.numpy as jnp
from jax import lax
from jax.experimental import pallas as pl
from jax.experimental.pallas import tpu as pltpu
from jax.sharding import PartitionSpec as P

epsilon = 1e-06
score_scale = 168.0 ** (-0.5)
window = 1024
vmem_limit = 58_000_000
MESH = pl.DeviceIdType.MESH
halves_of = ((0, 0), (1, 2), (2, 1), (3, 3))


def column_step(total, limit):
    step = 128
    for count in range(1, limit // 128 + 1):
        if total % (count * 128) == 0:
            step = count * 128
    return step


def layer_kernel(
    n_ctx, reach, q_heads, kv_heads, head, o_step,
    tok_hbm, wq_hbm, wk_hbm, wv_hbm, wo_hbm, pre_hbm, post_hbm, qg_hbm, kg_hbm,
    out_ref,
    w, wo, nb, nrm, raw, q, kv, att, pb, rx, ry, dg, small, gains, pre, post, cos, sin, accs, sums,
    load_sem, ag_s, ag_r, un_s, un_r, dc_s, dc_r, dr_s, dr_r, cb_s, cb_r, z_s, z_r, b_s, b_r, z_ready,
):
    f = lax.axis_index("fsdp")
    c = lax.axis_index("ctx")
    quarter, features = nb.shape[3:]
    half, rows = 2 * quarter, 4 * quarter
    z = c // 2
    p = c % 2
    nz = n_ctx // 2
    x_to = {"fsdp": f + 1 - 2 * (f % 2)}
    y_to = {"fsdp": (f + 2) % 4}
    sib = {"ctx": c + 1 - 2 * p}

    def ahead(step):
        return {"ctx": lax.rem(c + 2 * step, n_ctx)}, z + step < nz

    def behind(step):
        return {"ctx": lax.rem(c + n_ctx - 2 * step, n_ctx)}, z >= step

    direct = [step for step in (1, 3) if step <= reach]
    qw, kw = q_heads * head, kv_heads * head
    group = q_heads // kv_heads

    barrier = pltpu.get_barrier_semaphore()
    for to in (x_to, y_to, sib):
        pl.semaphore_signal(barrier, inc=1, device_id=to, device_id_type=MESH)
    peers, readers = 3, 0
    for step in direct:
        to, there = ahead(step)
        pl.when(there)(functools.partial(
            pl.semaphore_signal, barrier, inc=1, device_id=to, device_id_type=MESH
        ))
        peers = peers + jnp.clip(z - step + 1, 0, 1)
        readers = readers + jnp.clip(nz - z - step, 0, 1)

    def load(i, src, dst):
        return pltpu.make_async_copy(src, dst, load_sem.at[i])

    tok_load = load(0, tok_hbm, nb.at[0])
    small_loads = [
        load(1, pre_hbm, small.at[0]), load(2, post_hbm, small.at[1]),
        load(3, qg_hbm, gains.at[0]), load(4, kg_hbm, gains.at[1]),
    ]
    cut = features // 2
    w_loads = []
    for j, (src, lo, wide) in enumerate(((wk_hbm, qw, kw), (wv_hbm, qw + kw, kw), (wq_hbm, 0, qw))):
        for part in range(2):
            rs = pl.ds(part * cut, cut)
            w_loads.append(load(5 + 2 * j + part, src.at[rs], w.at[rs, pl.ds(lo, wide)]))
    wo_load = load(11, wo_hbm, wo)
    for d in [tok_load] + small_loads + w_loads + [wo_load]:
        d.start()

    def remote(src, dst, s, r, to):
        return pltpu.make_async_remote_copy(
            src_ref=src, dst_ref=dst, send_sem=s, recv_sem=r, device_id=to, device_id_type=MESH
        )

    def ag(link, k):
        part, h = k // 2, k % 2
        a = (link, 1 - link, 1 - link)[part]
        src = tok_hbm.at[a, h] if part < 2 else nb.at[1, a, h]
        return remote(src, nb.at[part + 1, a, h], ag_s.at[link, k], ag_r.at[link, k], (x_to, y_to)[link])

    pl.semaphore_wait(barrier, peers)
    for k in range(4):
        for link in range(2):
            ag(link, k).start()
    for step in direct:
        to, there = behind(step)
        pl.when(there)(functools.partial(
            pl.semaphore_signal, z_ready, inc=1, device_id=to, device_id_type=MESH
        ))

    r = lax.broadcasted_iota(jnp.int32, (rows, head), 0)
    lane = lax.broadcasted_iota(jnp.int32, (rows, head), 1)
    at_row = c * rows + (r // quarter) % 2 * half + r // half * quarter + r % quarter
    which = (lane % (head // 2)).astype(jnp.float32)
    angles = at_row.astype(jnp.float32) * jnp.exp(which * (-math.log(10000.0) / (head // 2)))
    cos[...] = jnp.cos(angles)
    sin[...] = jnp.where(lane < head // 2, -1.0, 1.0) * jnp.sin(angles)

    for d in small_loads:
        d.wait()
    for wide, i in ((pre, 0), (post, 1)):
        wide[...] = jnp.concatenate([small[i, k : k + 1, :] for k in range(small.shape[1])], axis=1)

    def norm(u, h):
        def body(i, carry):
            a, at = i // (quarter // 16), pl.ds(pl.multiple_of(i % (quarter // 16) * 16, 16), 16)
            v = nb[u, a, h, at, :].astype(jnp.float32)
            mean_sq = jnp.mean(v * v, axis=-1, keepdims=True)
            to = pl.ds(pl.multiple_of(h * half + i * 16, 16), 16)
            nrm[to, :] = (v * lax.rsqrt(mean_sq + epsilon) * pre[...]).astype(jnp.bfloat16)
            return carry

        lax.fori_loop(0, half // 16, body, 0)

    def z_copy(u, h, dz, step):
        return remote(
            kv.at[u, dz, p, :, h], kv.at[u, dz + step, p, :, h],
            z_s.at[u, h, dz + step], z_r.at[u, h, dz + step], ahead(step)[0],
        )

    def b_copy(u, h, dz):
        return remote(kv.at[u, dz, p, :, h], kv.at[u, dz, p, :, h], b_s.at[u, h, dz], b_r.at[u, h, dz], sib)

    def kv_arrived(u, h, dz):
        at = kv.at[u, dz, p, :, h]
        return remote(at, at, z_s.at[u, h, dz], z_r.at[u, h, dz], behind(1)[0])

    def kv_paired(u, h, dz):
        at = kv.at[u, dz, 1 - p, :, h]
        return remote(at, at, b_s.at[u, h, dz], b_r.at[u, h, dz], sib)

    def own_copies(u, h, act):
        for step in direct:
            @pl.when(ahead(step)[1])
            def _():
                act(z_copy(u, h, 0, step))

        @pl.when(p == 0)
        def _():
            act(b_copy(u, h, 0))

    def send_own(u, h):
        own_copies(u, h, lambda d: d.start())

    def passed_copies(u, h, dz, act):
        if dz in direct and dz + 1 <= reach:
            @pl.when(ahead(1)[1])
            def _():
                act(z_copy(u, h, dz, 1))

        act(b_copy(u, h, dz))

    def relay(u, h, dz):
        if dz > reach:
            return

        @pl.when(z >= dz)
        def _():
            kv_arrived(u, h, dz).wait_recv()
            passed_copies(u, h, dz, lambda d: d.start())

    def relay_rest(u, h):
        for dz in range(2, reach + 1):
            relay(u, h, dz)

    def wait_pairs(u):
        for h in range(2):
            @pl.when(p == 1)
            def _():
                kv_paired(u, h, 0).wait_recv()

            for dz in range(1, reach + 1):
                @pl.when(z >= dz)
                def _():
                    kv_paired(u, h, dz).wait_recv()

    k_step = column_step(2 * kw, 256)
    q_step = column_step(qw, 256)

    def columns_of(lo, size, first, count, step):
        def columns(j, carry):
            at = pl.ds(pl.multiple_of(first + j * step, 128), step)
            raw[lo : lo + size, at] = jnp.dot(nrm[lo : lo + size, :], w[:, at], preferred_element_type=jnp.float32)
            return carry

        lax.fori_loop(0, count // step, columns, 0)

    def rotated(lo, size, col, gain):
        v = raw[lo : lo + size, col : col + head]
        mean_sq = jnp.mean(v * v, axis=-1, keepdims=True)
        v = v * lax.rsqrt(mean_sq + epsilon) * gain
        v = v * cos[lo : lo + size, :] + pltpu.roll(v, head // 2, 1) * sin[lo : lo + size, :]
        return v.astype(jnp.bfloat16)

    def project_keys(u, h):
        lo = h * half
        columns_of(lo, half, qw, 2 * kw, k_step)
        for g in range(kv_heads):
            keys = rotated(lo, half, qw + g * head, gains[1])
            for a in range(2):
                kv[u, 0, p, a, h, :, g * head : (g + 1) * head] = keys[a * quarter : (a + 1) * quarter]
        for a in range(2):
            at = slice(lo + a * quarter, lo + (a + 1) * quarter)
            kv[u, 0, p, a, h, :, kw:] = raw[at, qw + kw :].astype(jnp.bfloat16)

    def project_queries(u):
        columns_of(0, rows, 0, qw, q_step)
        for g in range(q_heads):
            found = rotated(0, rows, g * head, gains[0])
            for h in range(2):
                for a in range(2):
                    to, at = a * half + h * quarter, (2 * h + a) * quarter
                    q[u, to : to + quarter, g * head : (g + 1) * head] = found[at : at + quarter]

    def merged(parts):
        return jnp.concatenate(parts, axis=0)

    def attend(u):
        own, other = halves_of[u], halves_of[(0, 2, 1, 3)[u]]
        spans = [(0, rows, own)] if own == other else [(0, half, own), (half, half, other)]
        streams = [
            (i * kv_heads + g, g, lo, size, units)
            for i, (lo, size, units) in enumerate(spans) for g in range(kv_heads)
        ]

        def places(lo, size):
            qi = lax.broadcasted_iota(jnp.int32, (group, size, rows), 1).reshape(group * size, rows) + lo
            return qi, lax.broadcasted_iota(jnp.int32, (group * size, rows), 1)

        def block(units, dz, par, cols):
            return merged([
                kv[units[a], dz, par, a, h, :, cols] for a in range(2) for h in range(2)
            ])

        def step(dz, pars, mask, first=False):
            for n, g, lo, size, units in streams:
                kc = slice(g * head, (g + 1) * head)
                vc = slice(kw + g * head, kw + (g + 1) * head)
                at = slice(0, group * size)
                queries = merged([
                    q[u, lo : lo + size, h * head : (h + 1) * head] for h in range(g * group, (g + 1) * group)
                ])
                keys = merged([block(units, dz, par, kc) for par in pars])
                values = merged([block(units, dz, par, vc) for par in pars])
                s = lax.dot_general(queries, keys, (((1,), (1,)), ((), ())), preferred_element_type=jnp.float32)
                e = jnp.exp(s * score_scale)
                if mask is not None:
                    e = jnp.where(mask(lo, size), e, 0.0)
                total = sum(e[:, i * rows : (i + 1) * rows] for i in range(len(pars)))
                acc = jnp.dot(e.astype(jnp.bfloat16), values, preferred_element_type=jnp.float32)
                if first:
                    sums[n, at], accs[n, at] = total, acc
                else:
                    sums[n, at] += total
                    accs[n, at] += acc

        def causal(lo, size):
            qi, kj = places(lo, size)
            return kj <= qi

        step(0, [p], causal, True)

        def beside(_, carry):
            step(0, [0], None)
            return carry

        def earlier(dz, carry):
            def near(lo, size):
                qi, kj = places(lo, size)
                apart = (p + 2 * dz) * rows + qi - kj
                return jnp.concatenate([apart, apart - rows], axis=1) < window

            step(dz, [0, 1], near if n_ctx * rows > window else None)
            return carry

        lax.fori_loop(0, p, beside, 0)
        lax.fori_loop(1, jnp.minimum(z, reach) + 1, earlier, 0)
        for n, g, lo, size, _ in streams:
            at = slice(0, group * size)
            o = (accs[n, at] / jnp.sum(sums[n, at], axis=-1, keepdims=True)).astype(jnp.bfloat16)
            for i in range(group):
                h = g * group + i
                att[u, lo : lo + size, h * head : (h + 1) * head] = o[i * size : (i + 1) * size]

    blocks = features // o_step

    def output(u, send=None):
        def columns(j, carry):
            at = pl.ds(pl.multiple_of(j * o_step, o_step), o_step)
            pb[u, :, at] = jnp.dot(att[u], wo[:, at], preferred_element_type=jnp.float32).astype(jnp.bfloat16)
            if send is not None:
                pl.when(j > 0)(lambda: send(j - 1))
            return carry

        lax.fori_loop(0, blocks, columns, 0)
        if send is not None:
            send(blocks - 1)

    def unit_copy(link, j):
        at = (pl.ds(link * half, half), pl.ds(pl.multiple_of(j * o_step, o_step), o_step))
        return remote(
            pb.at[(1, *at)], (rx, ry)[link].at[at], un_s.at[link, j], un_r.at[link, j], (x_to, y_to)[link]
        )

    def far_columns(link, j):
        at = (pl.ds(link * half, quarter), pl.ds(pl.multiple_of(j * o_step, o_step), o_step))
        return remote(pb.at[(3, *at)], dg.at[at], dc_s.at[link, j], dc_r.at[link, j], (x_to, y_to)[link])

    def far_rows(link, i):
        at = pl.ds(link * half + quarter + i * 16, 16)
        return remote(pb.at[3, at], dg.at[at], dr_s.at[link, i], dr_r.at[link, i], (x_to, y_to)[link])

    def sum_copy(link, i):
        at = pl.ds((1 - link) * half + i * 16, 16)
        return remote(pb.at[2, at], (rx, ry)[link].at[at], cb_s.at[link, i], cb_r.at[link, i], (x_to, y_to)[link])

    def both(copy, i, act="start"):
        for link in range(2):
            getattr(copy(link, i), act)()

    def every(copy, count, act):
        def body(j, carry):
            both(copy, j, act)
            return carry

        lax.fori_loop(0, count, body, 0)

    def add_rows(at):
        pb[2, at, :] = (pb[2, at, :].astype(jnp.float32) + dg[at, :].astype(jnp.float32)).astype(jnp.bfloat16)

    def arrive(u, h):
        both(ag, 2 * (u - 1) + h, "wait_recv")
        if u == 1:
            both(ag, 4 + h)
        norm(u, h)
        project_keys(u, h)

    tok_load.wait()
    norm(0, 0)
    norm(0, 1)
    for d in w_loads[:4]:
        d.wait()
    project_keys(0, 0)
    project_keys(0, 1)
    for d in w_loads[4:]:
        d.wait()
    project_queries(0)
    arrive(1, 0)
    pl.when(readers > 0)(lambda: pl.semaphore_wait(z_ready, readers))
    send_own(1, 0)
    arrive(1, 1)
    send_own(1, 1)
    relay(1, 0, 1)
    project_queries(1)
    relay(1, 1, 1)
    arrive(2, 0)
    send_own(2, 0)
    relay_rest(1, 0)
    wo_load.wait()
    arrive(2, 1)
    send_own(2, 1)
    relay(2, 0, 1)
    relay_rest(1, 1)
    project_queries(2)
    relay(2, 1, 1)
    relay_rest(2, 0)
    arrive(3, 0)
    send_own(3, 0)
    relay_rest(2, 1)
    wait_pairs(1)
    wait_pairs(2)
    attend(1)
    output(1, lambda j: both(unit_copy, j))
    arrive(3, 1)
    send_own(3, 1)
    relay(3, 0, 1)
    project_queries(3)
    attend(2)
    relay(3, 1, 1)
    relay_rest(3, 0)
    send_own(0, 0)
    send_own(0, 1)
    output(2)
    relay_rest(3, 1)
    wait_pairs(3)
    attend(3)
    output(3, lambda j: both(far_columns, j))
    for i in range(quarter // 16):
        both(far_rows, i)
    relay(0, 0, 1)
    relay(0, 1, 1)

    every(far_columns, blocks, "wait_recv")
    tiles = half // 16
    for i in range(tiles):
        if i >= tiles // 2:
            both(far_rows, i - tiles // 2, "wait_recv")
        for a in range(2):
            add_rows(pl.ds(a * half + i * 16, 16))
        both(sum_copy, i)
    relay_rest(0, 0)
    relay_rest(0, 1)
    wait_pairs(0)
    attend(0)
    output(0)

    every(unit_copy, blocks, "wait_recv")
    for i in range(tiles):
        both(sum_copy, i, "wait_recv")
        for a in range(2):
            at = pl.ds(a * half + i * 16, 16)
            summed = pb[0, at, :].astype(jnp.float32) + rx[at, :].astype(jnp.float32) + ry[at, :].astype(jnp.float32)
            mean_sq = jnp.mean(summed * summed, axis=-1, keepdims=True)
            normed = summed * lax.rsqrt(mean_sq + epsilon) * post[...]
            mine = nb[0, a, i * 16 // quarter, pl.ds(i * 16 % quarter, 16), :].astype(jnp.float32)
            out_ref[at, :] = (mine + normed).astype(jnp.bfloat16)

    for k in range(6):
        both(ag, k, "wait_send")
    every(unit_copy, blocks, "wait_send")
    every(far_columns, blocks, "wait_send")
    for i in range(quarter // 16):
        both(far_rows, i, "wait_send")
    for i in range(tiles):
        both(sum_copy, i, "wait_send")
    for u in range(4):
        for h in range(2):
            own_copies(u, h, lambda d: d.wait_send())
            for dz in range(1, reach + 1):
                @pl.when(z >= dz)
                def _():
                    passed_copies(u, h, dz, lambda d: d.wait_send())


def per_device(
    n_ctx, tokens, pre_gain, w_query, key_weight, value_weight, query_norm_gain, key_gain, w_out, post_gain
):
    _, rows, features = tokens.shape
    head = query_norm_gain.shape[0]
    qw, kw = w_query.shape[1], key_weight.shape[1]
    reach = min(n_ctx // 2 - 1, -(-window // (2 * rows)))
    o_step = column_step(features, 768)
    blocks, tiles, quarter = features // o_step, rows // 32, rows // 4
    any_spec = pl.BlockSpec(memory_space=pl.ANY)
    bf16, f32 = jnp.bfloat16, jnp.float32
    dma = pltpu.SemaphoreType.DMA
    out = pl.pallas_call(
        functools.partial(layer_kernel, n_ctx, reach, qw // head, kw // head, head, o_step),
        out_shape=pltpu.VMEM((rows, features), bf16),
        in_specs=[any_spec] * 9,
        out_specs=pl.BlockSpec(memory_space=pltpu.VMEM),
        scratch_shapes=[
            pltpu.VMEM((features, qw + 2 * kw), bf16),
            pltpu.VMEM((qw, features), bf16),
            pltpu.VMEM((4, 2, 2, quarter, features), bf16),
            pltpu.VMEM((rows, features), bf16),
            pltpu.VMEM((rows, qw + 2 * kw), f32),
            pltpu.VMEM((4, rows, qw), bf16),
            pltpu.VMEM((4, reach + 1, 2, 2, 2, quarter, 2 * kw), bf16),
            pltpu.VMEM((4, rows, qw), bf16),
            pltpu.VMEM((4, rows, features), bf16),
            pltpu.VMEM((rows, features), bf16),
            pltpu.VMEM((rows, features), bf16),
            pltpu.VMEM((rows, features), bf16),
            pltpu.VMEM((2, features // 128, 128), f32),
            pltpu.VMEM((2, 1, head), f32),
            pltpu.VMEM((1, features), f32),
            pltpu.VMEM((1, features), f32),
            pltpu.VMEM((rows, head), f32),
            pltpu.VMEM((rows, head), f32),
            pltpu.VMEM((2 * kw // head, qw // kw * rows, head), f32),
            pltpu.VMEM((2 * kw // head, qw // kw * rows, rows), f32),
            dma((12,)), dma((2, 6)), dma((2, 6)),
            dma((2, blocks)), dma((2, blocks)), dma((2, blocks)), dma((2, blocks)),
            dma((2, tiles // 2)), dma((2, tiles // 2)), dma((2, tiles)), dma((2, tiles)),
            dma((4, 2, reach + 1)), dma((4, 2, reach + 1)), dma((4, 2, reach + 1)), dma((4, 2, reach + 1)),
            pltpu.SemaphoreType.REGULAR,
        ],
        compiler_params=pltpu.CompilerParams(
            collective_id=0, has_side_effects=True, vmem_limit_bytes=vmem_limit
        ),
    )(
        tokens.reshape(2, 2, quarter, features), w_query, key_weight, value_weight, w_out,
        pre_gain.reshape(-1, 128), post_gain.reshape(-1, 128), query_norm_gain[None], key_gain[None],
    )
    return out[None]


def solution(mesh):
    return jax.shard_map(
        functools.partial(per_device, mesh.shape["ctx"]),
        mesh=mesh,
        in_specs=(
            P("fsdp", "ctx", None),
            P(),
            P(None, "fsdp"),
            P(None, "fsdp"),
            P(None, "fsdp"),
            P(),
            P(),
            P("fsdp", None),
            P(),
        ),
        out_specs=P("fsdp", "ctx", None),
        check_vma=False,
    )
```

time: 111 us -> 108 us (0.973)
  local copies, waits for them, and re-layouts: 2.51 us -> 1.08 us
    unnamed x1, local copies, waits for them, and re-layouts: 2.51 us -> 1.08 us
where the time goes in v1:
time: 108 us
  Pallas kernels  106 us (98%)
  local copies, waits for them, and re-layouts  1.08 us (1%)
    pallas_call x1, Pallas kernels, per_device(): pl.pallas_call(functools.partial(layer_kernel, n_ctx, reach, qw // head,...  106 us

profile of v1, /device:TPU:24, one launch (start us, length us, event | category | flops | bytes accessed | tf_op | source)
XLA Modules:
  0.0 107.6 jit_solution(8537771650973643725)
XLA Ops:
  0.0 106.5 %shard_map.91 = bf16[128,5376]{1,0:T(8,128)(2,1)S(1)} custom-call(bf16[2,2,32,5376]{3,2,1,0:T(8,128)(2,1)} %bitcast.7, bf16[5376,768]{1,0:T(8,128)(2,1)} %wq_hbm.1, bf16[5376,384]{1,0:T(8,128)(2,1)} %wk_hbm.1, bf16[5376,384]{1,0:T(8,128)(2,1)} %wv_hbm.1, bf16[768,5376]{1,0:T(8,128)(2,1)} %wo_hbm.1, f32[42,128]{1,0:T(8,128)} %bitcast.8, f32[42,128]{1,0:T(8,128)} %bitcast.9, ...), custom_call_target="tpu_custom_call" | custom-call | tf_op jit(solution)/shard_map/pallas_call | solution.py:462
  106.5 1.1 %copy.11 = bf16[1,128,5376]{2,1,0:T(8,128)(2,1)} copy(bf16[1,128,5376]{2,1,0:T(8,128)(2,1)S(1)} %bitcast.6) | data formatting | bytes 2752512

commit v2 on v1

--- a/solution.py
+++ b/solution.py
@@ -174,20 +174,21 @@
             kv_arrived(u, h, dz).wait_recv()
             passed_copies(u, h, dz, lambda d: d.start())
 
-    def relay_rest(u, h):
-        for dz in range(2, reach + 1):
-            relay(u, h, dz)
-
-    def wait_pairs(u):
-        for h in range(2):
-            @pl.when(p == 1)
-            def _():
-                kv_paired(u, h, 0).wait_recv()
-
-            for dz in range(1, reach + 1):
-                @pl.when(z >= dz)
-                def _():
-                    kv_paired(u, h, dz).wait_recv()
+    farthest = jnp.minimum(z, reach)
+
+    def share(units, dz):
+        for u in units:
+            for h in range(2):
+                kv_arrived(u, h, dz).wait_recv()
+                for step in direct:
+                    if step > 1 and step + 1 <= reach:
+                        pl.when((dz == step) & ahead(1)[1])(z_copy(u, h, step, 1).start)
+                b_copy(u, h, dz).start()
+
+    def wait_pairs(units, dz):
+        for u in units:
+            for h in range(2):
+                kv_paired(u, h, dz).wait_recv()
 
     k_step = column_step(2 * kw, 256)
     q_step = column_step(qw, 256)
@@ -230,7 +231,7 @@
     def merged(parts):
         return jnp.concatenate(parts, axis=0)
 
-    def attend(u):
+    def attention(u, fresh):
         own, other = halves_of[u], halves_of[(0, 2, 1, 3)[u]]
         spans = [(0, rows, own)] if own == other else [(0, half, own), (half, half, other)]
         streams = [
@@ -273,11 +274,15 @@
             qi, kj = places(lo, size)
             return kj <= qi
 
-        step(0, [p], causal, True)
-
-        def beside(_, carry):
-            step(0, [0], None)
-            return carry
+        def begin():
+            step(0, [p], causal, True)
+
+            def beside(_, carry):
+                wait_pairs(fresh, 0)
+                step(0, [0], None)
+                return carry
+
+            lax.fori_loop(0, p, beside, 0)
 
         def earlier(dz, carry):
             def near(lo, size):
@@ -285,21 +290,29 @@
                 apart = (p + 2 * dz) * rows + qi - kj
                 return jnp.concatenate([apart, apart - rows], axis=1) < window
 
+            pl.when(dz + 1 <= farthest)(lambda: share(fresh, dz + 1))
+            wait_pairs(fresh, dz)
             step(dz, [0, 1], near if n_ctx * rows > window else None)
             return carry
 
-        lax.fori_loop(0, p, beside, 0)
-        lax.fori_loop(1, jnp.minimum(z, reach) + 1, earlier, 0)
-        for n, g, lo, size, _ in streams:
-            at = slice(0, group * size)
-            o = (accs[n, at] / jnp.sum(sums[n, at], axis=-1, keepdims=True)).astype(jnp.bfloat16)
-            for i in range(group):
-                h = g * group + i
-                att[u, lo : lo + size, h * head : (h + 1) * head] = o[i * size : (i + 1) * size]
+        def complete():
+            lax.fori_loop(1, farthest + 1, earlier, 0)
+            for n, g, lo, size, _ in streams:
+                at = slice(0, group * size)
+                o = (accs[n, at] / jnp.sum(sums[n, at], axis=-1, keepdims=True)).astype(jnp.bfloat16)
+                for i in range(group):
+                    h = g * group + i
+                    att[u, lo : lo + size, h * head : (h + 1) * head] = o[i * size : (i + 1) * size]
+
+        return begin, complete
+
+    def attend(u, fresh):
+        for part in attention(u, fresh):
+            part()
 
     blocks = features // o_step
 
-    def output(u, send=None):
+    def output(u, send=None, first=0, last=blocks):
         def columns(j, carry):
             at = pl.ds(pl.multiple_of(j * o_step, o_step), o_step)
             pb[u, :, at] = jnp.dot(att[u], wo[:, at], preferred_element_type=jnp.float32).astype(jnp.bfloat16)
@@ -307,8 +320,8 @@
                 pl.when(j > 0)(lambda: send(j - 1))
             return carry
 
-        lax.fori_loop(0, blocks, columns, 0)
-        if send is not None:
+        lax.fori_loop(first, last, columns, 0)
+        if send is not None and last == blocks:
             send(blocks - 1)
 
     def unit_copy(link, j):
@@ -343,12 +356,15 @@
     def add_rows(at):
         pb[2, at, :] = (pb[2, at, :].astype(jnp.float32) + dg[at, :].astype(jnp.float32)).astype(jnp.bfloat16)
 
-    def arrive(u, h):
+    def arrive(u, h, between=None):
         both(ag, 2 * (u - 1) + h, "wait_recv")
         if u == 1:
             both(ag, 4 + h)
         norm(u, h)
+        if between is not None:
+            between()
         project_keys(u, h)
+        send_own(u, h)
 
     tok_load.wait()
     norm(0, 0)
@@ -356,54 +372,43 @@
     for d in w_loads[:4]:
         d.wait()
     project_keys(0, 0)
+    pl.when(readers > 0)(lambda: pl.semaphore_wait(z_ready, readers))
+    send_own(0, 0)
     project_keys(0, 1)
     for d in w_loads[4:]:
         d.wait()
     project_queries(0)
     arrive(1, 0)
-    pl.when(readers > 0)(lambda: pl.semaphore_wait(z_ready, readers))
-    send_own(1, 0)
+    relay(0, 0, 1)
     arrive(1, 1)
-    send_own(1, 1)
     relay(1, 0, 1)
     project_queries(1)
     relay(1, 1, 1)
     arrive(2, 0)
-    send_own(2, 0)
-    relay_rest(1, 0)
     wo_load.wait()
-    arrive(2, 1)
-    send_own(2, 1)
-    relay(2, 0, 1)
-    relay_rest(1, 1)
+    arrive(2, 1, lambda: relay(2, 0, 1))
     project_queries(2)
+    begin, complete = attention(1, (1, 2))
+    begin()
     relay(2, 1, 1)
-    relay_rest(2, 0)
     arrive(3, 0)
-    send_own(3, 0)
-    relay_rest(2, 1)
-    wait_pairs(1)
-    wait_pairs(2)
-    attend(1)
-    output(1, lambda j: both(unit_copy, j))
-    arrive(3, 1)
-    send_own(3, 1)
-    relay(3, 0, 1)
+    complete()
+    unit_send = lambda j: both(unit_copy, j)
+    early = min(3, blocks)
+    output(1, unit_send, 0, early)
+    arrive(3, 1, lambda: relay(3, 0, 1))
+    output(1, unit_send, early, blocks)
+    attend(2, ())
+    relay(3, 1, 1)
+    send_own(0, 1)
     project_queries(3)
-    attend(2)
-    relay(3, 1, 1)
-    relay_rest(3, 0)
-    send_own(0, 0)
-    send_own(0, 1)
-    output(2)
-    relay_rest(3, 1)
-    wait_pairs(3)
-    attend(3)
+    attend(3, (3,))
     output(3, lambda j: both(far_columns, j))
     for i in range(quarter // 16):
         both(far_rows, i)
-    relay(0, 0, 1)
     relay(0, 1, 1)
+    output(2)
+    attend(0, (0,))
 
     every(far_columns, blocks, "wait_recv")
     tiles = half // 16
@@ -413,10 +418,6 @@
         for a in range(2):
             add_rows(pl.ds(a * half + i * 16, 16))
         both(sum_copy, i)
-    relay_rest(0, 0)
-    relay_rest(0, 1)
-    wait_pairs(0)
-    attend(0)
     output(0)
 
     every(unit_copy, blocks, "wait_recv")

time: 108 us -> 102 us (0.944)
  Pallas kernels: 106 us -> 101 us
    pallas_call x1, Pallas kernels: 106 us -> 101 us  [per_device(): pl.pallas_call(functools.partial(layer_kernel, n_ctx, reach, qw // head,...]
where the time goes in v2:
time: 102 us
  Pallas kernels  101 us (99%)
  local copies, waits for them, and re-layouts  1.08 us (1%)
    pallas_call x1, Pallas kernels, per_device(): pl.pallas_call(functools.partial(layer_kernel, n_ctx, reach, qw // head,...  101 us

profile of v2, /device:TPU:24, one launch (start us, length us, event | category | flops | bytes accessed | tf_op | source)
XLA Modules:
  0.0 101.6 jit_solution(17660814351165615624)
XLA Ops:
  0.0 100.5 %shard_map.91 = bf16[128,5376]{1,0:T(8,128)(2,1)S(1)} custom-call(bf16[2,2,32,5376]{3,2,1,0:T(8,128)(2,1)} %bitcast.7, bf16[5376,768]{1,0:T(8,128)(2,1)} %wq_hbm.1, bf16[5376,384]{1,0:T(8,128)(2,1)} %wk_hbm.1, bf16[5376,384]{1,0:T(8,128)(2,1)} %wv_hbm.1, bf16[768,5376]{1,0:T(8,128)(2,1)} %wo_hbm.1, f32[42,128]{1,0:T(8,128)} %bitcast.8, f32[42,128]{1,0:T(8,128)} %bitcast.9, ...), custom_call_target="tpu_custom_call" | custom-call | tf_op jit(solution)/shard_map/pallas_call | solution.py:463
  100.6 1.1 %copy.11 = bf16[1,128,5376]{2,1,0:T(8,128)(2,1)} copy(bf16[1,128,5376]{2,1,0:T(8,128)(2,1)S(1)} %bitcast.6) | data formatting | bytes 2752512

commit v3 on v2

--- a/solution.py
+++ b/solution.py
@@ -25,7 +25,7 @@
 
 
 def layer_kernel(
-    n_ctx, reach, q_heads, kv_heads, head, o_step,
+    n_ctx, reach, q_heads, kv_heads, head, o_step, cuts,
     tok_hbm, wq_hbm, wk_hbm, wv_hbm, wo_hbm, pre_hbm, post_hbm, qg_hbm, kg_hbm,
     out_ref,
     w, wo, nb, nrm, raw, q, kv, att, pb, rx, ry, dg, small, gains, pre, post, cos, sin, accs, sums,
@@ -284,13 +284,18 @@
 
             lax.fori_loop(0, p, beside, 0)
 
-        def earlier(dz, carry):
+        def order(k):
+            return jnp.where(k == 1, 1, farthest + 2 - k)
+
+        def earlier(k, carry):
+            dz = order(k)
+
             def near(lo, size):
                 qi, kj = places(lo, size)
                 apart = (p + 2 * dz) * rows + qi - kj
                 return jnp.concatenate([apart, apart - rows], axis=1) < window
 
-            pl.when(dz + 1 <= farthest)(lambda: share(fresh, dz + 1))
+            pl.when(k < farthest)(lambda: share(fresh, order(k + 1)))
             wait_pairs(fresh, dz)
             step(dz, [0, 1], near if n_ctx * rows > window else None)
             return carry
@@ -312,26 +317,24 @@
 
     blocks = features // o_step
 
-    def output(u, send=None, first=0, last=blocks):
+    def output(u, first=0, last=blocks):
         def columns(j, carry):
             at = pl.ds(pl.multiple_of(j * o_step, o_step), o_step)
             pb[u, :, at] = jnp.dot(att[u], wo[:, at], preferred_element_type=jnp.float32).astype(jnp.bfloat16)
-            if send is not None:
-                pl.when(j > 0)(lambda: send(j - 1))
             return carry
 
         lax.fori_loop(first, last, columns, 0)
-        if send is not None and last == blocks:
-            send(blocks - 1)
+
+    spread = [pl.ds(i * o_step, (j - i) * o_step) for i, j in zip(cuts[:-1], cuts[1:])]
 
     def unit_copy(link, j):
-        at = (pl.ds(link * half, half), pl.ds(pl.multiple_of(j * o_step, o_step), o_step))
+        at = (pl.ds(link * half, half), spread[j])
         return remote(
             pb.at[(1, *at)], (rx, ry)[link].at[at], un_s.at[link, j], un_r.at[link, j], (x_to, y_to)[link]
         )
 
     def far_columns(link, j):
-        at = (pl.ds(link * half, quarter), pl.ds(pl.multiple_of(j * o_step, o_step), o_step))
+        at = (pl.ds(link * half, quarter), spread[j])
         return remote(pb.at[(3, *at)], dg.at[at], dc_s.at[link, j], dc_r.at[link, j], (x_to, y_to)[link])
 
     def far_rows(link, i):
@@ -347,11 +350,18 @@
             getattr(copy(link, i), act)()
 
     def every(copy, count, act):
-        def body(j, carry):
-            both(copy, j, act)
-            return carry
-
-        lax.fori_loop(0, count, body, 0)
+        for i in range(count):
+            both(copy, i, act)
+
+    def output_and_send(u, copy, between=None):
+        done = 0
+        for i, stop in enumerate(cuts[1:]):
+            upto = min(stop + 1, blocks)
+            output(u, done, upto)
+            both(copy, i)
+            done = upto
+            if i == 0 and between is not None:
+                between()
 
     def add_rows(at):
         pb[2, at, :] = (pb[2, at, :].astype(jnp.float32) + dg[at, :].astype(jnp.float32)).astype(jnp.bfloat16)
@@ -393,24 +403,20 @@
     relay(2, 1, 1)
     arrive(3, 0)
     complete()
-    unit_send = lambda j: both(unit_copy, j)
-    early = min(3, blocks)
-    output(1, unit_send, 0, early)
-    arrive(3, 1, lambda: relay(3, 0, 1))
-    output(1, unit_send, early, blocks)
+    output_and_send(1, unit_copy, lambda: arrive(3, 1, lambda: relay(3, 0, 1)))
     attend(2, ())
     relay(3, 1, 1)
     send_own(0, 1)
     project_queries(3)
     attend(3, (3,))
-    output(3, lambda j: both(far_columns, j))
+    output_and_send(3, far_columns)
     for i in range(quarter // 16):
         both(far_rows, i)
     relay(0, 1, 1)
     output(2)
     attend(0, (0,))
 
-    every(far_columns, blocks, "wait_recv")
+    every(far_columns, len(spread), "wait_recv")
     tiles = half // 16
     for i in range(tiles):
         if i >= tiles // 2:
@@ -420,7 +426,7 @@
         both(sum_copy, i)
     output(0)
 
-    every(unit_copy, blocks, "wait_recv")
+    every(unit_copy, len(spread), "wait_recv")
     for i in range(tiles):
         both(sum_copy, i, "wait_recv")
         for a in range(2):
@@ -433,8 +439,8 @@
 
     for k in range(6):
         both(ag, k, "wait_send")
-    every(unit_copy, blocks, "wait_send")
-    every(far_columns, blocks, "wait_send")
+    every(unit_copy, len(spread), "wait_send")
+    every(far_columns, len(spread), "wait_send")
     for i in range(quarter // 16):
         both(far_rows, i, "wait_send")
     for i in range(tiles):
@@ -457,11 +463,13 @@
     reach = min(n_ctx // 2 - 1, -(-window // (2 * rows)))
     o_step = column_step(features, 768)
     blocks, tiles, quarter = features // o_step, rows // 32, rows // 4
+    cuts = sorted({0, min(3, blocks), blocks})
+    ranges = len(cuts) - 1
     any_spec = pl.BlockSpec(memory_space=pl.ANY)
     bf16, f32 = jnp.bfloat16, jnp.float32
     dma = pltpu.SemaphoreType.DMA
     out = pl.pallas_call(
-        functools.partial(layer_kernel, n_ctx, reach, qw // head, kw // head, head, o_step),
+        functools.partial(layer_kernel, n_ctx, reach, qw // head, kw // head, head, o_step, cuts),
         out_shape=pltpu.VMEM((rows, features), bf16),
         in_specs=[any_spec] * 9,
         out_specs=pl.BlockSpec(memory_space=pltpu.VMEM),
@@ -487,7 +495,7 @@
             pltpu.VMEM((2 * kw // head, qw // kw * rows, head), f32),
             pltpu.VMEM((2 * kw // head, qw // kw * rows, rows), f32),
             dma((12,)), dma((2, 6)), dma((2, 6)),
-            dma((2, blocks)), dma((2, blocks)), dma((2, blocks)), dma((2, blocks)),
+            dma((2, ranges)), dma((2, ranges)), dma((2, ranges)), dma((2, ranges)),
             dma((2, tiles // 2)), dma((2, tiles // 2)), dma((2, tiles)), dma((2, tiles)),
             dma((4, 2, reach + 1)), dma((4, 2, reach + 1)), dma((4, 2, reach + 1)), dma((4, 2, reach + 1)),
             pltpu.SemaphoreType.REGULAR,

time: 102 us -> 101 us (level)
  Pallas kernels: 101 us -> 99.8 us
where the time goes in v3:
time: 101 us
  Pallas kernels  99.8 us (99%)
  local copies, waits for them, and re-layouts  1.08 us (1%)
    pallas_call x1, Pallas kernels, per_device(): pl.pallas_call(functools.partial(layer_kernel, n_ctx, reach, qw // head,...  99.8 us

profile of v3, /device:TPU:24, one launch (start us, length us, event | category | flops | bytes accessed | tf_op | source)
XLA Modules:
  0.0 100.9 jit_solution(15827972558226732911)
XLA Ops:
  0.0 99.8 %shard_map.91 = bf16[128,5376]{1,0:T(8,128)(2,1)S(1)} custom-call(bf16[2,2,32,5376]{3,2,1,0:T(8,128)(2,1)} %bitcast.7, bf16[5376,768]{1,0:T(8,128)(2,1)} %wq_hbm.1, bf16[5376,384]{1,0:T(8,128)(2,1)} %wk_hbm.1, bf16[5376,384]{1,0:T(8,128)(2,1)} %wv_hbm.1, bf16[768,5376]{1,0:T(8,128)(2,1)} %wo_hbm.1, f32[42,128]{1,0:T(8,128)} %bitcast.8, f32[42,128]{1,0:T(8,128)} %bitcast.9, ...), custom_call_target="tpu_custom_call" | custom-call | tf_op jit(solution)/shard_map/pallas_call | solution.py:471
  99.8 1.1 %copy.11 = bf16[1,128,5376]{2,1,0:T(8,128)(2,1)} copy(bf16[1,128,5376]{2,1,0:T(8,128)(2,1)S(1)} %bitcast.6) | data formatting | bytes 2752512

commit v4 on v3

--- a/solution.py
+++ b/solution.py
@@ -414,7 +414,6 @@
         both(far_rows, i)
     relay(0, 1, 1)
     output(2)
-    attend(0, (0,))
 
     every(far_columns, len(spread), "wait_recv")
     tiles = half // 16
@@ -424,6 +423,7 @@
         for a in range(2):
             add_rows(pl.ds(a * half + i * 16, 16))
         both(sum_copy, i)
+    attend(0, (0,))
     output(0)
 
     every(unit_copy, len(spread), "wait_recv")

time: 101 us -> 101 us (level)
  no operation moved by 1% of the time
where the time goes in v4:
time: 101 us
  Pallas kernels  99.8 us (99%)
  local copies, waits for them, and re-layouts  1.08 us (1%)
    pallas_call x1, Pallas kernels, per_device(): pl.pallas_call(functools.partial(layer_kernel, n_ctx, reach, qw // head,...  99.8 us

profile of v4, /device:TPU:24, one launch (start us, length us, event | category | flops | bytes accessed | tf_op | source)
XLA Modules:
  0.0 100.9 jit_solution(11202102198898052116)
XLA Ops:
  0.0 99.8 %shard_map.91 = bf16[128,5376]{1,0:T(8,128)(2,1)S(1)} custom-call(bf16[2,2,32,5376]{3,2,1,0:T(8,128)(2,1)} %bitcast.7, bf16[5376,768]{1,0:T(8,128)(2,1)} %wq_hbm.1, bf16[5376,384]{1,0:T(8,128)(2,1)} %wk_hbm.1, bf16[5376,384]{1,0:T(8,128)(2,1)} %wv_hbm.1, bf16[768,5376]{1,0:T(8,128)(2,1)} %wo_hbm.1, f32[42,128]{1,0:T(8,128)} %bitcast.8, f32[42,128]{1,0:T(8,128)} %bitcast.9, ...), custom_call_target="tpu_custom_call" | custom-call | tf_op jit(solution)/shard_map/pallas_call | solution.py:471
  99.8 1.1 %copy.11 = bf16[1,128,5376]{2,1,0:T(8,128)(2,1)} copy(bf16[1,128,5376]{2,1,0:T(8,128)(2,1)S(1)} %bitcast.6) | data formatting | bytes 2752512
